TPU v7x, 32 devices: a whole 2x2x4 slice. The times are simulated.
32 devices in a mesh: groups: 2 (over y), tensor: 4 (over z), dp: 4 (over x, core).
Axes of the slice: x: 2, y: 2, z: 4, core: 2. Of those that a mesh axis runs over, the one named last changes fastest.
Arguments:
- tokens: bfloat16 [256, 8192], P(('groups', 'tensor', 'dp')), parts along dimension 0, may hold values from -6 to 6
- gate_projection_matrix: bfloat16 [8192, 14336], P('dp', 'tensor'), may hold values from -0.0625 to 0.0625
- up_projection_matrix: bfloat16 [8192, 14336], P('dp', 'tensor'), may hold values from -0.0625 to 0.0625
- down_projection_matrix: bfloat16 [14336, 8192], P('tensor', 'dp'), may hold values from -0.046875 to 0.046875
- gate_adapter_inmap: bfloat16 [16384, 64], P(('groups', 'dp')), parts along dimension 0, may hold values from -0.0625 to 0.0625
- gate_adapter_outmap: bfloat16 [64, 28672], P(None, ('groups', 'tensor')), parts along dimension 1, may hold values from -0.75 to 0.75
- up_adapter_inmap: bfloat16 [16384, 64], P(('groups', 'dp')), parts along dimension 0, may hold values from -0.0625 to 0.0625
- up_adapter_outmap: bfloat16 [64, 28672], P(None, ('groups', 'tensor')), parts along dimension 1, may hold values from -0.75 to 0.75
- down_adapter_inmap: bfloat16 [28672, 64], P(('groups', 'tensor')), parts along dimension 0, may hold values from -0.046875 to 0.046875
- down_adapter_outmap: bfloat16 [64, 16384], P(None, 'groups'), parts along dimension 1, may hold values from -0.75 to 0.75
Outputs:
- block_out: bfloat16 [256, 8192], P(('groups', 'tensor', 'dp')), parts along dimension 0
There are 2 independent parts, one for each index of `groups`. A program takes and returns all parts, laid end to end along the dimension named above; an argument that names none is the same for every part. Nothing has to cross between parts.
All inputs are finite; a program needn't handle non-finite values.
Results may differ from a plain program's by a relative error of at most 0.0053.
Values may be sent and summed in bfloat16 or wider, within the bound.
A program may use at most 256 MiB of HBM per device.

v0:
```python
import jax
import jax.numpy as jnp
from jax import lax
from jax.sharding import PartitionSpec as P

adapter_scale_factor = 0.5


def body(
    tokens,
    gate_projection_matrix,
    up_projection_matrix,
    down_projection_matrix,
    gate_adapter_inmap,
    gate_adapter_outmap,
    up_adapter_inmap,
    up_adapter_outmap,
    down_adapter_inmap,
    down_adapter_outmap,
):
    tok_dev = tokens.shape[0]
    n_tensor = lax.axis_size("tensor")
    n_dp = lax.axis_size("dp")
    hidden_unit_count = gate_projection_matrix.shape[1]
    adapter_rank_size = gate_adapter_inmap.shape[1]
    columns = lax.all_to_all(tokens, "dp", split_axis=1, concat_axis=0, tiled=True)
    stacked_lowrank = jnp.concatenate(
        [gate_projection_matrix, up_projection_matrix, gate_adapter_inmap, up_adapter_inmap], axis=1
    )
    partial_all = jnp.dot(
        lax.all_gather(columns, "tensor", axis=0, tiled=True),
        stacked_lowrank,
        preferred_element_type=jnp.float32,
    )
    partial_all = partial_all.reshape(n_tensor, n_dp, tok_dev, partial_all.shape[1])
    summed_lowrank = lax.psum_scatter(partial_all, "dp", scatter_dimension=1, tiled=True)
    summed_lowrank = summed_lowrank.reshape(n_tensor * tok_dev, summed_lowrank.shape[3])
    gate_dense_part = summed_lowrank[:, :hidden_unit_count]
    up_dense_part = summed_lowrank[:, hidden_unit_count : 2 * hidden_unit_count]
    gate_lowrank_part = summed_lowrank[
        :, 2 * hidden_unit_count : 2 * hidden_unit_count + adapter_rank_size
    ].astype(jnp.bfloat16)
    up_lowrank_part = summed_lowrank[:, 2 * hidden_unit_count + adapter_rank_size :].astype(
        jnp.bfloat16
    )
    gate_activated = gate_dense_part + adapter_scale_factor * jnp.dot(
        gate_lowrank_part, gate_adapter_outmap, preferred_element_type=jnp.float32
    )
    up_projected_value = up_dense_part + adapter_scale_factor * jnp.dot(
        up_lowrank_part, up_adapter_outmap, preferred_element_type=jnp.float32
    )
    hidden_product = (jax.nn.silu(gate_activated) * up_projected_value).astype(jnp.bfloat16)
    down_outmap_single = down_adapter_outmap.astype(jnp.float32)
    lowrank_term_list = jnp.dot(
        hidden_product, down_adapter_inmap, preferred_element_type=jnp.float32
    )
    owned_lowrank_part = lax.psum_scatter(
        lowrank_term_list, "tensor", scatter_dimension=0, tiled=True
    )
    term = jnp.dot(
        hidden_product,
        lax.all_gather(down_projection_matrix, "dp", axis=1, tiled=True),
        preferred_element_type=jnp.float32,
    )
    block_result_rows = lax.psum_scatter(term, "tensor", scatter_dimension=0, tiled=True)
    block_result_rows = block_result_rows + adapter_scale_factor * jnp.dot(
        owned_lowrank_part, down_outmap_single, precision=lax.Precision.HIGHEST
    )
    return block_result_rows.astype(jnp.bfloat16)


def solution(mesh):
    placed = (
        P(("groups", "tensor", "dp"), None),
        P("dp", "tensor"),
        P("dp", "tensor"),
        P("tensor", "dp"),
        P(("groups", "dp"), None),
        P(None, ("groups", "tensor")),
        P(("groups", "dp"), None),
        P(None, ("groups", "tensor")),
        P(("groups", "tensor"), None),
        P(None, "groups"),
    )
    return jax.shard_map(
        body,
        mesh=mesh,
        in_specs=placed,
        out_specs=P(("groups", "tensor", "dp"), None),
        check_vma=False,
    )
```

profile of v0, /device:TPU:0, one launch (start us, length us, event | category | flops | bytes accessed | tf_op | source)
XLA Modules:
  0.0 576.1 jit_solution(376535880790217102)
XLA Ops:
  6.5 0.0 copy-start
  6.5 4.4 all-to-all-start
  10.9 0.0 all-reduce.4.cloned.1.call-start
  10.9 1.2 copy.13
  12.1 1.2 copy.14
  13.4 44.4 %concatenate.3 = bf16[2048,7296]{1,0:T(8,128)(2,1)} concatenate(bf16[2048,3584]{1,0:T(8,128)(2,1)} %param.11, bf16[2048,3584]{1,0:T(8,128)(2,1)} %param.12, bf16[2048,64]{1,0:T(8,128)(2,1)S(1)} %copy.13, bf16[2048,64]{1,0:T(8,128)(2,1)S(1)} %copy.14), dimensions={1} | concatenate | bytes 59768832 | tf_op jit(solution)/shard_map/concatenate | solution.py:27
  57.8 0.0 all-to-all-done
  57.8 17.1 %all_gather.6 = bf16[128,2048]{1,0:T(8,128)(2,1)S(1)} all-gather(bf16[32,2048]{1,0:T(8,128)(2,1)S(1)} %bitcast.24), channel_id=1, replica_groups=mesh['groups'=2,'tensor'=4,'dp'=4] {'tensor'}, dimensions={0}, use_global_device_ids=true | all-gather | bytes 655360 | tf_op jit(solution)/shard_map/all_gather | solution.py:31
  74.9 15.4 %fusion.13 = f32[7296,128]{0,1:T(8,128)} fusion(bf16[128,2048]{1,0:T(8,128)(2,1)S(1)} %all_gather.6, bf16[2048,7296]{1,0:T(8,128)(2,1)} %concatenate.3), kind=kOutput, calls=%fused_computation.17 | convolution fusion | flops 3825205248 | bytes 34144256 | tf_op jit(solution)/shard_map/dot_general | solution.py:30
  90.3 0.0 all-reduce.4.cloned.1.call-update
  90.3 0.0 all-gather.2.cloned.1.call-start
  90.4 0.7 all-gather.2.cloned.1.call-update
  91.1 0.0 reduce-scatter.3.cloned.1.call-start
  91.2 0.0 copy-done.5
  91.2 0.6 dynamic-slice
  91.7 78.5 %all-reduce.4.cloned.1.call-done = f32[4,4,8,7296]{3,2,1,0:T(8,128)} async-done(((f32[4,4,8,7296]{3,2,1,0:T(8,128)}), f32[4,4,8,7296]{3,2,1,0:T(8,128)}) %all-reduce.4.cloned.1.call-update) | async-done | bytes 3735568
  170.2 1.9 fusion.10
  172.2 0.0 copy-done.2
  172.2 0.2 fusion.4
  172.4 0.0 copy-done.3
  172.4 0.3 fusion.5
  172.7 0.0 copy-start.4
  172.7 0.0 copy-start.1
  172.7 345.2 %all-gather.2.cloned.1.call-done = bf16[3584,8192]{1,0:T(8,128)(2,1)} async-done(((bf16[3584,2048]{1,0:T(8,128)(2,1)}), bf16[3584,8192]{1,0:T(8,128)(2,1)}) %all-gather.2.cloned.1.call-update) | async-done | bytes 58720272 | tf_op jit(solution)/shard_map/all_gather | solution.py:62
  518.0 21.6 %fusion.11 = f32[32,8192]{1,0:T(8,128)} fusion(bf16[32,3584]{1,0:T(8,128)(2,1)S(1)} %fusion.5, bf16[3584,8192]{1,0:T(8,128)(2,1)} %all-gather.2.cloned.1.call-done), kind=kOutput, calls=%fused_computation.15 | convolution fusion | flops 1879048192 | bytes 59998208 | tf_op jit(solution)/shard_map/dot_general | solution.py:60
  539.6 0.0 reduce-scatter.3.cloned.1.call-update
  539.6 0.6 dynamic-slice.2
  540.9 0.2 fusion.12
  541.1 19.7 %all-reduce.1 = f32[32,64]{1,0:T(8,128)S(1)} all-reduce(f32[32,64]{1,0:T(8,128)S(1)} %fusion.12), channel_id=4, replica_groups=mesh['groups'=2,'tensor'=4,'dp'=4] {'tensor'}, use_global_device_ids=true, to_apply=%region_2.3.clone | all-reduce | flops 2048 | bytes 16384
  560.9 6.6 %reduce-scatter.3.cloned.1.call-done = f32[8,8192]{1,0:T(8,128)} async-done(((f32[32,8192]{1,0:T(8,128)}), f32[8,8192]{1,0:T(8,128)}) %reduce-scatter.3.cloned.1.call-update) | async-done | bytes 262160 | tf_op jit(solution)/shard_map/reduce_scatter | solution.py:65
  567.4 0.0 copy-done
  567.4 2.1 fusion.1
  (5 shorter events, 0.0 us)
Async XLA Ops:
  6.5 560.9 %copy-start = (bf16[64,8192]{1,0:T(8,128)(2,1)S(1)}, bf16[64,8192]{1,0:T(8,128)(2,1)}, u32[]{:S(2)}) copy-start(bf16[64,8192]{1,0:T(8,128)(2,1)} %param.19) | copy-start | bytes 3145732
  6.5 51.2 %all-to-all-start = ((bf16[8,4,2048]{2,0,1:T(8,128)(2,1)}), bf16[8,4,2048]{2,0,1:T(8,128)(2,1)S(1)}, u32[]{:S(2)}, u32[]{:S(2)}) async-start(bf16[8,4,2048]{2,0,1:T(8,128)(2,1)} %bitcast.25), calls=%async_computation | async-start | bytes 262144 | tf_op jit(solution)/shard_map/all_to_all | solution.py:26
  10.9 159.3 %all-reduce.4.cloned.1.call-start = ((), (), s32[]{:S(2)}) async-start(), calls=%async_computation.4 | async-start | bytes 7471104
  57.7 33.4 %copy-start.5 = (u32[32]{0:T(128)S(1)}, u32[32]{0:T(128)}, u32[]{:S(2)}) copy-start(u32[32]{0:T(128)} %constant.9) | copy-start | bytes 388
  57.8 114.4 %copy-start.2 = (bf16[64,3584]{1,0:T(8,128)(2,1)S(1)}, bf16[64,3584]{1,0:T(8,128)(2,1)}, u32[]{:S(2)}) copy-start(bf16[64,3584]{1,0:T(8,128)(2,1)} %param.15) | copy-start | bytes 1376260
  57.8 114.6 %copy-start.3 = (bf16[64,3584]{1,0:T(8,128)(2,1)S(1)}, bf16[64,3584]{1,0:T(8,128)(2,1)}, u32[]{:S(2)}) copy-start(bf16[64,3584]{1,0:T(8,128)(2,1)} %param.17) | copy-start | bytes 1376260
  90.3 427.6 %all-gather.2.cloned.1.call-start = ((), (), s32[]{:S(2)}) async-start(), calls=%async_computation.2 | async-start | bytes 73400320 | tf_op jit(solution)/shard_map/all_gather | solution.py:62
  91.1 476.3 %reduce-scatter.3.cloned.1.call-start = ((), (), s32[]{:S(2)}) async-start(), calls=%async_computation.3 | async-start | bytes 1310720 | tf_op jit(solution)/shard_map/reduce_scatter | solution.py:65
  172.7 366.9 %copy-start.4 = (u32[32]{0:T(128)S(1)}, u32[32]{0:T(128)}, u32[]{:S(2)}) copy-start(u32[32]{0:T(128)} %constant.13) | copy-start | bytes 388
  172.7 368.2 %copy-start.1 = (bf16[3584,64]{0,1:T(8,128)(2,1)S(1)}, bf16[3584,64]{0,1:T(8,128)(2,1)}, u32[]{:S(2)}) copy-start(bf16[3584,64]{0,1:T(8,128)(2,1)} %param.18) | copy-start | bytes 1376260
Sparse Core Ops, SparseCore 0:
  90.5 79.7 all-reduce.3
  171.8 346.1 all-gather.1
  539.8 27.6 reduce-scatter.2
where the time goes:
time: 578 us; the launch traced here: 576 us
  waiting for transfers between devices  431 us (75%)
  local copies, waits for them, and re-layouts  48 us (8%)
  matrix products  39.9 us (7%)
  blocking collectives  36.9 us (6%)
  between operations  13.9 us (2%)
    all_gather x1, waiting for transfers between devices, body(): lax.all_gather(down_projection_matrix, 'dp', axis=1, tiled=True)  345 us
    unnamed x4, waiting for transfers between devices  79.2 us
    concatenate x1, local copies, waits for them, and re-layouts, body(): jnp.concatenate([gate_projection_matrix, up_projection_matrix, gate_adapt...  44.4 us
    dot_general x1, matrix products, body(): jnp.dot(hidden_product, lax.all_gather(down_projection_matrix, 'dp', axis...  21.6 us
    unnamed x1, blocking collectives  19.7 us
    all_gather x1, blocking collectives, body(): lax.all_gather(columns, 'tensor', axis=0, tiled=True)  17.1 us
    dot_general x1, matrix products, body(): jnp.dot(lax.all_gather(columns, 'tensor', axis=0, tiled=True), stacked_lo...  15.4 us
  transfers between devices with their start and end apart: 4, of which 3 were waited for; matrix products, arithmetic and copies ran while one was open for 9% of the time, Pallas kernels for 0%

commit v1 on v0

--- a/solution.py
+++ b/solution.py
@@ -59,7 +59,10 @@
     )
     term = jnp.dot(
         hidden_product,
-        lax.all_gather(down_projection_matrix, "dp", axis=1, tiled=True),
+        jnp.concatenate(
+            lax.all_to_all(jnp.stack([down_projection_matrix] * lax.axis_size("dp")), "dp", 0, 0),
+            axis=1,
+        ),
         preferred_element_type=jnp.float32,
     )
     block_result_rows = lax.psum_scatter(term, "tensor", scatter_dimension=0, tiled=True)

time: 578 us -> 823 us (1.42)
  waiting for transfers between devices: 431 us -> 619 us
  local copies, waits for them, and re-layouts: 48 us -> 88.4 us
  starting transfers between devices: 4.45 us -> 17.1 us
    all_to_all x0 -> x1, waiting for transfers between devices: none -> 472 us  [body(): lax.all_to_all(jnp.stack([down_projection_matrix] * lax.axis_size('dp')),...]
    all_gather x1 -> x0, waiting for transfers between devices: 345 us -> none  [body(): lax.all_gather(down_projection_matrix, 'dp', axis=1, tiled=True)]
    unnamed x4 -> x3, waiting for transfers between devices: 79.2 us -> 140 us
    another operation x0 -> x1, local copies, waits for them, and re-layouts: none -> 23.4 us  [body(): jnp.stack([down_projection_matrix] * lax.axis_size('dp'))]
    unnamed x16 -> x21, local copies, waits for them, and re-layouts: 3.65 us -> 20.5 us
    all_to_all x0 -> x1, starting transfers between devices: none -> 12.6 us  [body(): lax.all_to_all(jnp.stack([down_projection_matrix] * lax.axis_size('dp')),...]
  transfers between devices with their start and end apart: 4 -> 4, of which waited for: 3 -> 3; matrix products, arithmetic and copies ran while one was open for 9% -> 10% of each run, Pallas kernels for 0% -> 0%
where the time goes in v1:
time: 823 us; the launch traced here: 821 us
  waiting for transfers between devices  619 us (75%)
  local copies, waits for them, and re-layouts  88.4 us (11%)
  matrix products  43.2 us (5%)
  blocking collectives  37.4 us (5%)
  starting transfers between devices  17.1 us (2%)
  between operations  14.2 us (2%)
    all_to_all x1, waiting for transfers between devices, body(): lax.all_to_all(jnp.stack([down_projection_matrix] * lax.axis_size('dp')),...  472 us
    unnamed x3, waiting for transfers between devices  140 us
    concatenate x1, local copies, waits for them, and re-layouts, body(): jnp.concatenate([gate_projection_matrix, up_projection_matrix, gate_adapt...  44.5 us
    dot_general x1, matrix products, body(): jnp.dot(hidden_product, jnp.concatenate(lax.all_to_all(jnp.stack([down_pr...  25 us
    another operation x1, local copies, waits for them, and re-layouts, body(): jnp.stack([down_projection_matrix] * lax.axis_size('dp'))  23.4 us
    unnamed x21, local copies, waits for them, and re-layouts  20.5 us
    unnamed x1, blocking collectives  20.3 us
    all_gather x1, blocking collectives, body(): lax.all_gather(columns, 'tensor', axis=0, tiled=True)  17.1 us
  transfers between devices with their start and end apart: 4, of which 3 were waited for; matrix products, arithmetic and copies ran while one was open for 10% of the time, Pallas kernels for 0%

profile of v1, /device:TPU:0, one launch (start us, length us, event | category | flops | bytes accessed | tf_op | source)
XLA Modules:
  0.0 820.8 jit_solution(10929038281734506860)
XLA Ops:
  6.5 0.0 copy-start
  6.5 4.4 all-to-all-start
  10.9 18.8 %copy.18 = bf16[3584,2048]{0,1:T(8,128)(2,1)} copy(bf16[3584,2048]{1,0:T(8,128)(2,1)} %param.13) | data formatting | bytes 29360128 | tf_op args[3]
  29.7 0.0 all-to-all-done
  29.7 23.4 %stack.2 = bf16[4,3584,2048]{1,2,0:T(8,128)(2,1)} broadcast(bf16[3584,2048]{0,1:T(8,128)(2,1)} %copy.18), dimensions={1,2} | broadcast | bytes 73400320 | tf_op jit(solution)/shard_map/stack | solution.py:63
  53.1 12.6 %all-to-all-start.1 = ((bf16[4,3584,2048]{1,2,0:T(8,128)(2,1)}), bf16[4,3584,2048]{1,2,0:T(8,128)(2,1)}, u32[]{:S(2)}, u32[]{:S(2)}) async-start(bf16[4,3584,2048]{1,2,0:T(8,128)(2,1)} %stack.2), calls=%async_computation.1 | async-start | bytes 117440512 | tf_op jit(solution)/shard_map/all_to_all | solution.py:63
  65.7 0.0 all-reduce.4.cloned.1.call-start
  65.7 0.0 copy-done.3
  65.8 0.3 copy.16
  66.0 0.0 copy-done.4
  66.0 0.3 copy.17
  66.3 44.5 %concatenate.3 = bf16[2048,7296]{1,0:T(8,128)(2,1)} concatenate(bf16[2048,3584]{1,0:T(8,128)(2,1)} %param.11, bf16[2048,3584]{1,0:T(8,128)(2,1)} %param.12, bf16[2048,64]{1,0:T(8,128)(2,1)S(1)} %copy.16, bf16[2048,64]{1,0:T(8,128)(2,1)S(1)} %copy.17), dimensions={1} | concatenate | bytes 59768832 | tf_op jit(solution)/shard_map/concatenate | solution.py:27
  110.8 17.1 %all_gather.3 = bf16[128,2048]{1,0:T(8,128)(2,1)S(1)} all-gather(bf16[32,2048]{1,0:T(8,128)(2,1)S(1)} %bitcast.27), channel_id=1, replica_groups=mesh['groups'=2,'tensor'=4,'dp'=4] {'tensor'}, dimensions={0}, use_global_device_ids=true | all-gather | bytes 655360 | tf_op jit(solution)/shard_map/all_gather | solution.py:31
  127.9 15.4 %fusion.13 = f32[7296,128]{0,1:T(8,128)} fusion(bf16[128,2048]{1,0:T(8,128)(2,1)S(1)} %all_gather.3, bf16[2048,7296]{1,0:T(8,128)(2,1)} %concatenate.3), kind=kOutput, calls=%fused_computation.17 | convolution fusion | flops 3825205248 | bytes 34144256 | tf_op jit(solution)/shard_map/dot_general | solution.py:30
  143.3 0.0 all-reduce.4.cloned.1.call-update
  143.3 0.0 reduce-scatter.3.cloned.1.call-start
  143.4 0.0 copy-done.7
  143.4 0.6 dynamic-slice
  144.0 139.7 %all-reduce.4.cloned.1.call-done = f32[4,4,8,7296]{3,2,1,0:T(8,128)} async-done(((f32[4,4,8,7296]{3,2,1,0:T(8,128)}), f32[4,4,8,7296]{3,2,1,0:T(8,128)}) %all-reduce.4.cloned.1.call-update) | async-done | bytes 3735568
  283.7 1.9 fusion.10
  285.6 0.0 copy-done.2
  285.7 0.2 fusion.4
  285.9 0.3 fusion.5
  286.2 472.0 %all-to-all-done.1 = bf16[4,3584,2048]{1,2,0:T(8,128)(2,1)} async-done(((bf16[4,3584,2048]{1,2,0:T(8,128)(2,1)}), bf16[4,3584,2048]{1,2,0:T(8,128)(2,1)}, u32[]{:S(2)}, u32[]{:S(2)}) %all-to-all-start.1) | async-done | bytes 58720288 | tf_op jit(solution)/shard_map/all_to_all | solution.py:63
  758.2 25.0 %fusion.11 = f32[32,8192]{1,0:T(8,128)} fusion(bf16[32,3584]{1,0:T(8,128)(2,1)S(1)} %fusion.5, bf16[3584,8192]{0,1:T(8,128)(2,1)} %bitcast.7), kind=kOutput, calls=%fused_computation.15 | convolution fusion | flops 1879048192 | bytes 59998208 | tf_op jit(solution)/shard_map/dot_general | solution.py:60
  783.1 0.0 reduce-scatter.3.cloned.1.call-update
  783.2 0.6 dynamic-slice.2
  784.4 0.0 copy-done.1
  784.4 0.2 fusion.12
  784.7 20.3 %all-reduce.1 = f32[32,64]{1,0:T(8,128)S(1)} all-reduce(f32[32,64]{1,0:T(8,128)S(1)} %fusion.12), channel_id=4, replica_groups=mesh['groups'=2,'tensor'=4,'dp'=4] {'tensor'}, use_global_device_ids=true, to_apply=%region_2.3.clone | all-reduce | flops 2048 | bytes 16384
  804.9 6.9 reduce-scatter.3.cloned.1.call-done
  811.9 2.1 fusion.1
  (10 shorter events, 0.0 us)
Async XLA Ops:
  6.5 805.3 %copy-start = (bf16[64,8192]{1,0:T(8,128)(2,1)S(1)}, bf16[64,8192]{1,0:T(8,128)(2,1)}, u32[]{:S(2)}) copy-start(bf16[64,8192]{1,0:T(8,128)(2,1)} %param.19) | copy-start | bytes 3145732
  6.5 23.1 %all-to-all-start = ((bf16[8,4,2048]{2,0,1:T(8,128)(2,1)}), bf16[8,4,2048]{2,0,1:T(8,128)(2,1)S(1)}, u32[]{:S(2)}, u32[]{:S(2)}) async-start(bf16[8,4,2048]{2,0,1:T(8,128)(2,1)} %bitcast.28), calls=%async_computation | async-start | bytes 262144 | tf_op jit(solution)/shard_map/all_to_all | solution.py:26
  53.1 12.7 %copy-start.3 = (bf16[2048,64]{0,1:T(8,128)(2,1)S(1)}, bf16[2048,64]{0,1:T(8,128)(2,1)}, u32[]{:S(2)}) copy-start(bf16[2048,64]{0,1:T(8,128)(2,1)} %param.14) | copy-start | bytes 786436
  53.1 13.0 %copy-start.4 = (bf16[2048,64]{0,1:T(8,128)(2,1)S(1)}, bf16[2048,64]{0,1:T(8,128)(2,1)}, u32[]{:S(2)}) copy-start(bf16[2048,64]{0,1:T(8,128)(2,1)} %param.16) | copy-start | bytes 786436
  53.1 705.1 %all-to-all-start.1 = ((bf16[4,3584,2048]{1,2,0:T(8,128)(2,1)}), bf16[4,3584,2048]{1,2,0:T(8,128)(2,1)}, u32[]{:S(2)}, u32[]{:S(2)}) async-start(bf16[4,3584,2048]{1,2,0:T(8,128)(2,1)} %stack.2), calls=%async_computation.1 | async-start | bytes 117440512 | tf_op jit(solution)/shard_map/all_to_all | solution.py:63
  65.7 218.0 %all-reduce.4.cloned.1.call-start = ((), (), s32[]{:S(2)}) async-start(), calls=%async_computation.4 | async-start | bytes 7471104
  110.8 32.6 %copy-start.7 = (u32[32]{0:T(128)S(1)}, u32[32]{0:T(128)}, u32[]{:S(2)}) copy-start(u32[32]{0:T(128)} %constant.9) | copy-start | bytes 388
  110.8 174.9 %copy-start.2 = (bf16[64,3584]{1,0:T(8,128)(2,1)S(1)}, bf16[64,3584]{1,0:T(8,128)(2,1)}, u32[]{:S(2)}) copy-start(bf16[64,3584]{1,0:T(8,128)(2,1)} %param.15) | copy-start | bytes 1376260
  110.8 175.1 %copy-start.5 = (bf16[64,3584]{1,0:T(8,128)(2,1)S(1)}, bf16[64,3584]{1,0:T(8,128)(2,1)}, u32[]{:S(2)}) copy-start(bf16[64,3584]{1,0:T(8,128)(2,1)} %param.17) | copy-start | bytes 1376260
  143.3 668.5 %reduce-scatter.3.cloned.1.call-start = ((), (), s32[]{:S(2)}) async-start(), calls=%async_computation.3 | async-start | bytes 1310720 | tf_op jit(solution)/shard_map/reduce_scatter | solution.py:68
  758.2 25.0 %copy-start.6 = (u32[32]{0:T(128)S(1)}, u32[32]{0:T(128)}, u32[]{:S(2)}) copy-start(u32[32]{0:T(128)} %constant.13) | copy-start | bytes 388
  758.2 26.2 %copy-start.1 = (bf16[3584,64]{0,1:T(8,128)(2,1)S(1)}, bf16[3584,64]{0,1:T(8,128)(2,1)}, u32[]{:S(2)}) copy-start(bf16[3584,64]{0,1:T(8,128)(2,1)} %param.18) | copy-start | bytes 1376260
Sparse Core Ops, SparseCore 0:
  143.4 140.2 all-reduce.3
  783.3 28.5 reduce-scatter.2
